TPU v7x, 32 devices: a whole 2x2x4 slice. The times are simulated.
32 devices in a mesh: section: 4 (over z), dp: 4 (over x, core), mp: 2 (over y).
Axes of the slice: x: 2, y: 2, z: 4, core: 2. Of those that a mesh axis runs over, the one named last changes fastest.
Arguments:
- hidden: bfloat16 [4, 16, 4, 4096], P('section', 'mp', 'dp'), may hold values from -2048 to 2048
- token_ids: int32 [16, 4], P('mp', 'dp'), may hold values from 0 to 8191
- seq_lengths: int32 [4], replicated, may hold values from 1 to 16, 21 in all
- head_slices: bfloat16 [4, 4096, 8192], P('section', None, ('dp', 'mp')), may hold values from -8 to 8
- value_head: bfloat16 [4, 4096], P('section'), may hold values from -0.09375 to 0.09375
Outputs:
- scores: float32 [4, 16, 4], P('section', 'mp', 'dp')
- advantages: float32 [16, 4], P('mp', 'dp')
- trunk_grad: bfloat16 [4, 16, 4, 4096], P('section', 'mp', 'dp')
Inputs may be any that keep to these rules, and one draw needn't show every extreme that they name: Sequence j is live at positions 0 to seq_lengths[j] - 1; the lengths sum to 21 and one of them is 16.
All inputs are finite; a program needn't handle non-finite values.
Results may differ from a plain program's by a relative error of at most 0.0047.
Values may be sent and summed in bfloat16 or wider, within the bound.
A program may use at most 64 MiB of HBM per device.

v0:
```python
import math
import jax
import jax.numpy as jnp
from jax import lax
from jax.sharding import PartitionSpec as P

gae_decay = 0.95
reward_gain = 0.5
drift_gain = 0.1
penalty_gain = 0.2
loss_scale = 16.0


def from_root(value, axis, source):
    kept = jnp.where(lax.axis_index(axis) == source, value, 0).astype(value.dtype)
    return lax.psum(kept, axis)


def joined(x, axis, combine):
    everything = jax.tree.map(lambda part: lax.all_gather(part, axis), x)
    first = jax.tree.map(lambda part: part[0], everything)

    def turn(k, so_far):
        return combine(so_far, jax.tree.map(lambda part: part[k], everything))

    return lax.fori_loop(1, lax.axis_size(axis), turn, first)


def block_logits(gathered, head_part):
    return jnp.dot(gathered, head_part, preferred_element_type=jnp.float32)


def merge_parts(earlier_part, later_part):
    maximum = jnp.maximum(earlier_part[0], later_part[0])
    exp_total = earlier_part[1] * jnp.exp(earlier_part[0] - maximum) + later_part[1] * jnp.exp(
        later_part[0] - maximum
    )
    return (maximum, exp_total, earlier_part[2] + later_part[2])


def local(hidden, token_ids, seq_lengths, head_slices, value_head):
    sections = lax.axis_size("section")
    per_device = hidden.shape[1]
    model_width = hidden.shape[3]
    vocab_part = head_slices.shape[2]
    seq_count = seq_lengths.shape[0]
    length = per_device * lax.axis_size("mp")
    head_part = head_slices[0]
    critic_head = value_head[0]
    own_block = from_root(hidden, "section", 0)
    gathered, row_ids = (
        lax.all_gather(own_block[0, :, 0, :], ("dp", "mp"), axis=0, tiled=True),
        lax.all_gather(token_ids[:, 0], ("dp", "mp"), axis=0, tiled=True),
    )
    row_total = gathered.shape[0]
    row_iota = lax.broadcasted_iota(jnp.int32, (row_total,), 0)
    seq_of = row_iota // length
    pos_of = row_iota % length
    seq_table = lax.broadcasted_iota(jnp.int32, (row_total, seq_count), 1)
    length_of = jnp.sum(jnp.where(seq_of[:, None] == seq_table, seq_lengths[None, :], 0), axis=1)
    live_bool = pos_of < length_of
    live_mask = live_bool.astype(jnp.float32)
    logits = block_logits(gathered, head_part)
    own_index = lax.axis_index("dp") * lax.axis_size("mp") + lax.axis_index("mp")
    vocab_start = own_index * vocab_part
    column = lax.broadcasted_iota(jnp.int32, logits.shape, 1) + vocab_start
    maximum = jnp.max(logits, axis=1)
    exp_total = jnp.sum(jnp.exp(logits - maximum[:, None]), axis=1)
    picked = jnp.sum(jnp.where(column == row_ids[:, None], logits, jnp.float32(0.0)), axis=1)
    values = jnp.dot(gathered, critic_head, preferred_element_type=jnp.float32)
    maximum, exp_total, picked = joined((maximum, exp_total, picked), ("dp", "mp"), merge_parts)
    normal = maximum + jnp.log(exp_total)
    scored = jnp.where(live_bool, picked - normal, jnp.float32(0.0))
    own_start = own_index * per_device
    scores_out = lax.dynamic_slice_in_dim(scored, own_start, per_device, 0).reshape(
        1, per_device, 1
    )
    joined_scores, joined_values = (
        lax.all_gather(scored[None, :], "section", axis=0, tiled=True),
        lax.all_gather(values[None, :], "section", axis=0, tiled=True),
    )
    behaviour = joined_scores[0]
    implicit = joined_scores[1]
    anchor = joined_scores[2]
    current = joined_scores[3]
    reward = (reward_gain * (implicit - anchor) - drift_gain * (behaviour - anchor)).reshape(
        seq_count, length
    )
    critic_grid = joined_values[1].reshape(seq_count, length)
    live_grid = live_mask.reshape(seq_count, length)
    next_values = jnp.concatenate(
        [critic_grid[:, 1:], jnp.zeros((seq_count, 1), jnp.float32)], axis=1
    )
    next_mask = jnp.concatenate([live_grid[:, 1:], jnp.zeros((seq_count, 1), jnp.float32)], axis=1)
    td_error = live_grid * (reward + next_mask * next_values - critic_grid)
    later_pos = lax.broadcasted_iota(jnp.int32, (length, length), 0)
    earlier = lax.broadcasted_iota(jnp.int32, (length, length), 1)
    weights_t = jnp.where(
        later_pos >= earlier,
        jnp.exp((later_pos - earlier).astype(jnp.float32) * math.log(gae_decay)),
        jnp.float32(0.0),
    )
    advantage = jnp.dot(td_error, weights_t, precision=lax.Precision.HIGHEST).reshape(row_total)
    advantage_out = lax.dynamic_slice_in_dim(advantage, own_start, per_device, 0).reshape(
        per_device, 1
    )
    prob_ratio = jnp.exp(current - behaviour)
    token_grad = (
        -(loss_scale / seq_count)
        * live_mask
        * (prob_ratio * advantage - penalty_gain * (prob_ratio - 1.0))
    )
    soft_probs = jnp.exp(logits - normal[:, None])
    target_hit = (column == row_ids[:, None]).astype(jnp.float32)
    slope = (token_grad[:, None] * (target_hit - soft_probs)).astype(jnp.bfloat16)
    grad_rows = lax.psum_scatter(
        lax.dot_general(
            slope, head_part, (((1,), (1,)), ((), ())), preferred_element_type=jnp.float32
        ),
        ("dp", "mp"),
        scatter_dimension=0,
        tiled=True,
    )
    learner = (lax.axis_index("section") == sections - 1).astype(jnp.float32)
    trunk_out = (grad_rows * learner).astype(jnp.bfloat16).reshape(1, per_device, 1, model_width)
    return (scores_out, advantage_out, trunk_out)


def solution(mesh):
    return jax.shard_map(
        local,
        mesh=mesh,
        in_specs=(
            P("section", "mp", "dp", None),
            P("mp", "dp"),
            P(),
            P("section", None, ("dp", "mp")),
            P("section", None),
        ),
        out_specs=(P("section", "mp", "dp"), P("mp", "dp"), P("section", "mp", "dp", None)),
        check_vma=False,
    )
```

profile of v0, /device:TPU:0, one launch (start us, length us, event | category | flops | bytes accessed | tf_op | source)
XLA Modules:
  0.0 146.0 jit_solution(6107833239940460607)
XLA Ops:
  7.2 1.5 %select_bitcast_fusion = bf16[8,4096]{1,0:T(8,128)(2,1)} fusion(bf16[1,8,1,4096]{3,1,2,0:T(8,128)(2,1)} %param.7, pred[]{:T(512)S(6)} %eq.30), kind=kLoop, calls=%fused_computation.28 | loop fusion | flops 32768 | bytes 131073 | tf_op jit(solution)/shard_map/squeeze | solution.py:52
  8.8 1.2 dynamic-slice.4
  10.1 1.2 dynamic-slice
  13.2 0.8 bitcast_dynamic-update-slice_fusion
  14.0 8.8 %all-reduce.4 = s32[64]{0:T(128)S(1)} all-reduce(s32[64]{0:T(128)S(1)} %bitcast_dynamic-update-slice_fusion), channel_id=4, replica_groups=mesh['section'=4,'dp'=4,'mp'=2] {'dp','mp'}, use_global_device_ids=true, to_apply=%add.4 | all-reduce | flops 64 | bytes 512
  22.8 0.7 select_reduce_fusion
  23.5 0.1 reduce_sum.32
  23.6 0.1 slice.37
  23.7 24.2 %all-reduce.12.cloned.1.call-done = bf16[8,4096]{1,0:T(8,128)(2,1)} async-done(((bf16[8,4096]{1,0:T(8,128)(2,1)}), bf16[8,4096]{1,0:T(8,128)(2,1)}) %all-reduce.12.cloned.1.call-update) | async-done | bytes 65552 | tf_op jit(solution)/shard_map/psum | solution.py:16
  47.9 16.6 %all_gather.30 = bf16[64,4096]{1,0:T(8,128)(2,1)S(1)} all-gather(bf16[8,4096]{1,0:T(8,128)(2,1)} %all-reduce.12.cloned.1.call-done), channel_id=1, replica_groups=mesh['section'=4,'dp'=4,'mp'=2] {'dp','mp'}, dimensions={0}, use_global_device_ids=true | all-gather | bytes 589824 | tf_op jit(solution)/shard_map/all_gather | solution.py:52
  64.5 5.1 %fusion.45 = (f32[64]{0:T(128)S(1)}, f32[64,1024]{1,0:T(8,128)S(1)}) fusion(bf16[64,4096]{1,0:T(8,128)(2,1)S(1)} %all_gather.30, bf16[1,4096,1024]{2,1,0:T(8,128)(2,1)} %param.10), kind=kOutput, calls=%fused_computation.72 | convolution fusion | flops 536936384 | bytes 9175296 | tf_op jit(solution)/shard_map/dot_general | solution.py:30
  69.5 0.2 dynamic-update-slice
  69.8 0.2 fusion.11
  70.0 0.2 dynamic-update-slice.3
  70.3 0.2 dynamic-update-slice.1
  70.5 14.3 %all-reduce.8 = (f32[512]{0:T(512)S(1)}, f32[512]{0:T(512)S(1)}, f32[512]{0:T(512)S(1)}) all-reduce(f32[512]{0:T(512)S(1)} %dynamic-update-slice, f32[512]{0:T(512)S(1)} %dynamic-update-slice.1, f32[512]{0:T(512)S(1)} %dynamic-update-slice.3), channel_id=2, replica_groups=mesh['section'=4,'dp'=4,'mp'=2] {'dp','mp'}, use_global_device_ids=true, to_apply=%add.2 | all-reduce | flops 1536 | bytes 12288
  84.7 0.1 reshape.90
  85.0 0.2 convolution_bitcast_fusion
  85.2 0.3 while.19
  85.5 0.2 dynamic-update-slice.5
  85.8 0.1 fusion.44
  85.9 10.4 %all-reduce.9 = (f32[256]{0:T(256)S(1)}, f32[256]{0:T(256)S(1)}) all-reduce(f32[256]{0:T(256)S(1)} %dynamic-update-slice.5, f32[256]{0:T(256)S(1)} %get-tuple-element.207), channel_id=7, replica_groups=mesh['section'=4,'dp'=4,'mp'=2] {'section'}, use_global_device_ids=true, to_apply=%add.7 | all-reduce | flops 512 | bytes 4096
  96.5 0.1 reshape_squeeze.3
  96.5 0.1 sub.97
  96.7 0.1 fusion.26
  96.8 0.1 reshape.84
  96.9 0.1 subtract_multiply_fusion
  97.0 7.1 %fusion.7 = f32[64,4096]{1,0:T(8,128)} fusion(bf16[1,4096,1024]{2,1,0:T(8,128)(2,1)} %param.10, f32[64,1024]{1,0:T(8,128)S(1)} %get-tuple-element.212, f32[64]{0:T(128)S(1)} %get-tuple-element.209, f32[64]{0:T(128)S(1)} %subtract_multiply_fusion, s32[1024]{0:T(1024)S(1)} %iota_add_fusion, s32[64]{0:T(128)S(1)} %all-reduce.4), kind=kOutput, calls=%fused_computation.10 | convolution fusion | flops 537264128 | bytes 9704192 | tf_op jit(solution)/shard_map/dot_general | solution.py:117
  104.1 0.6 dynamic-slice_bitcast_fusion
  104.7 0.6 dynamic-slice_bitcast_fusion.1
  105.3 32.4 %reduce-scatter.2.cloned.1.call-done = f32[8,4096]{1,0:T(8,128)} async-done(((f32[64,4096]{1,0:T(8,128)}), f32[8,4096]{1,0:T(8,128)}) %reduce-scatter.2.cloned.1.call-update) | async-done | bytes 131088 | tf_op jit(solution)/shard_map/reduce_scatter | solution.py:116
  137.7 1.5 %fusion.20 = bf16[1,8,1,4096]{3,1,2,0:T(8,128)(2,1)} fusion(f32[8,4096]{1,0:T(8,128)} %reduce-scatter.2.cloned.1.call-done, f32[]{:T(128)S(6)} %convert_element_type.22), kind=kLoop, calls=%fused_computation.27 | loop fusion | flops 65536 | bytes 196612 | tf_op jit(solution)/shard_map/reshape | solution.py:125
  (30 shorter events, 0.7 us)
Async XLA Ops:
  7.2 77.8 %copy-start = (bf16[1,4096]{1,0:T(2,128)(2,1)S(1)}, bf16[1,4096]{1,0:T(2,128)(2,1)}, u32[]{:S(2)}) copy-start(bf16[1,4096]{1,0:T(2,128)(2,1)} %param.11) | copy-start | bytes 24580
  7.2 40.7 %all-reduce.12.cloned.1.call-start = ((), (), s32[]{:S(2)}) async-start(), calls=%async_computation.1 | async-start | bytes 131072 | tf_op jit(solution)/shard_map/psum | solution.py:16
  8.7 128.9 %reduce-scatter.2.cloned.1.call-start = ((), (), s32[]{:S(2)}) async-start(), calls=%async_computation.2 | async-start | bytes 1179648 | tf_op jit(solution)/shard_map/reduce_scatter | solution.py:116
Sparse Core Ops, SparseCore 0:
  10.9 37.0 all-reduce.11
  104.2 33.4 reduce-scatter.1
where the time goes:
time: 146 us
  waiting for transfers between devices  56.6 us (39%)
  blocking collectives  50.1 us (34%)
  between operations  16 us (11%)
  matrix products  12.5 us (9%)
  local copies, waits for them, and re-layouts  6.16 us (4%)
  other arithmetic  4.46 us (3%)
    unnamed x3, blocking collectives  33.5 us
    reduce_scatter x1, waiting for transfers between devices, local(): lax.psum_scatter(lax.dot_general(slope, head_part, (((1,), (1,)), ((), ()...  32.4 us
    psum x1, waiting for transfers between devices, from_root(): return lax.psum(kept, axis)  24.2 us
    all_gather x1, blocking collectives, local(): lax.all_gather(own_block[0, :, 0, :], ('dp', 'mp'), axis=0, tiled=True)  16.6 us
    dot_general x1, matrix products, local(): lax.dot_general(slope, head_part, (((1,), (1,)), ((), ())), preferred_ele...  7.06 us
    dot_general x1, matrix products, block_logits(): return jnp.dot(gathered, head_part, preferred_element_type=jnp.float32)  5.06 us
    unnamed x14, local copies, waits for them, and re-layouts  4.19 us
  transfers between devices with their start and end apart: 2, of which 2 were waited for; matrix products, arithmetic and copies ran while one was open for 4% of the time, Pallas kernels for 0%

commit v1 on v0

--- a/solution.py
+++ b/solution.py
@@ -13,7 +13,7 @@
 
 def from_root(value, axis, source):
     kept = jnp.where(lax.axis_index(axis) == source, value, 0).astype(value.dtype)
-    return lax.psum(kept, axis)
+    return jnp.sum(lax.all_gather(kept, axis), axis=0)
 
 
 def joined(x, axis, combine):

time: 146 us -> 135 us (0.925)
  waiting for transfers between devices: 56.6 us -> 31.9 us
  blocking collectives: 50.1 us -> 64.9 us
    psum x1 -> x0, waiting for transfers between devices: 24.2 us -> none  [from_root(): return lax.psum(kept, axis)]
    all_gather x0 -> x1, blocking collectives: none -> 13.9 us  [from_root(): return jnp.sum(lax.all_gather(kept, axis), axis=0)]
    squeeze x1 -> x0, other arithmetic: 1.48 us -> none  [local(): own_block[0, :, 0, :]]
    unnamed x14 -> x18, local copies, waits for them, and re-layouts: 4.19 us -> 3.54 us
  transfers between devices with their start and end apart: 2 -> 1, of which waited for: 2 -> 1; matrix products, arithmetic and copies ran while one was open for 4% -> 1% of each run, Pallas kernels for 0% -> 0%
where the time goes in v1:
time: 135 us; the launch traced here: 134 us
  blocking collectives  64.9 us (48%)
  waiting for transfers between devices  31.9 us (24%)
  between operations  16.1 us (12%)
  matrix products  12.5 us (9%)
  local copies, waits for them, and re-layouts  5.5 us (4%)
  other arithmetic  3.21 us (2%)
    unnamed x3, blocking collectives  34.4 us
    reduce_scatter x1, waiting for transfers between devices, local(): lax.psum_scatter(lax.dot_general(slope, head_part, (((1,), (1,)), ((), ()...  31.9 us
    all_gather x1, blocking collectives, local(): lax.all_gather(own_block[0, :, 0, :], ('dp', 'mp'), axis=0, tiled=True)  16.6 us
    all_gather x1, blocking collectives, from_root(): return jnp.sum(lax.all_gather(kept, axis), axis=0)  13.9 us
    dot_general x1, matrix products, local(): lax.dot_general(slope, head_part, (((1,), (1,)), ((), ())), preferred_ele...  7.06 us
    dot_general x1, matrix products, block_logits(): return jnp.dot(gathered, head_part, preferred_element_type=jnp.float32)  5.08 us
    unnamed x18, local copies, waits for them, and re-layouts  3.54 us
  transfers between devices with their start and end apart: 1, of which 1 were waited for; matrix products, arithmetic and copies ran while one was open for 1% of the time, Pallas kernels for 0%

profile of v1, /device:TPU:0, one launch (start us, length us, event | category | flops | bytes accessed | tf_op | source)
XLA Modules:
  0.0 134.3 jit_solution(10524788118377774686)
XLA Ops:
  7.3 1.2 dynamic-slice
  9.8 0.8 bitcast_dynamic-update-slice_fusion
  10.6 8.8 %all-reduce.4 = s32[64]{0:T(128)S(1)} all-reduce(s32[64]{0:T(128)S(1)} %bitcast_dynamic-update-slice_fusion), channel_id=5, replica_groups=mesh['section'=4,'dp'=4,'mp'=2] {'dp','mp'}, use_global_device_ids=true, to_apply=%add.4 | all-reduce | flops 64 | bytes 512
  19.4 0.8 broadcast_select_fusion
  20.2 13.9 %all-gather = bf16[4,8,1,4096]{3,1,2,0:T(8,128)(2,1)S(1)} all-gather(bf16[1,8,1,4096]{3,1,2,0:T(8,128)(2,1)S(1)} %broadcast_select_fusion), channel_id=2, replica_groups=mesh['section'=4,'dp'=4,'mp'=2] {'section'}, dimensions={0}, use_global_device_ids=true | all-gather | bytes 327680 | tf_op jit(solution)/shard_map/all_gather | solution.py:16
  34.2 16.6 %all_gather.38 = bf16[64,4096]{1,0:T(8,128)(2,1)S(1)} all-gather(bf16[8,4096]{1,0:T(8,128)(2,1)S(1)} %reduce.2), channel_id=1, replica_groups=mesh['section'=4,'dp'=4,'mp'=2] {'dp','mp'}, dimensions={0}, use_global_device_ids=true | all-gather | bytes 589824 | tf_op jit(solution)/shard_map/all_gather | solution.py:52
  50.8 5.1 %fusion.45 = (f32[64]{0:T(128)S(1)}, f32[64,1024]{1,0:T(8,128)S(1)}) fusion(bf16[64,4096]{1,0:T(8,128)(2,1)S(1)} %all_gather.38, bf16[1,4096,1024]{2,1,0:T(8,128)(2,1)} %param.10), kind=kOutput, calls=%fused_computation.72 | convolution fusion | flops 536936384 | bytes 9175296 | tf_op jit(solution)/shard_map/dot_general | solution.py:30
  55.9 0.2 dynamic-update-slice
  56.2 0.2 fusion.11
  56.4 0.2 dynamic-update-slice.3
  56.6 0.2 dynamic-update-slice.1
  56.8 14.1 %all-reduce.8 = (f32[512]{0:T(512)S(1)}, f32[512]{0:T(512)S(1)}, f32[512]{0:T(512)S(1)}) all-reduce(f32[512]{0:T(512)S(1)} %dynamic-update-slice, f32[512]{0:T(512)S(1)} %dynamic-update-slice.1, f32[512]{0:T(512)S(1)} %dynamic-update-slice.3), channel_id=3, replica_groups=mesh['section'=4,'dp'=4,'mp'=2] {'dp','mp'}, use_global_device_ids=true, to_apply=%add.2 | all-reduce | flops 1536 | bytes 12288
  71.0 0.1 reshape.93
  71.2 0.6 dynamic-slice.4
  72.5 0.1 select_reduce_fusion
  72.6 0.1 reduce_sum.45
  72.7 0.1 slice.37
  72.7 0.2 convolution_bitcast_fusion
  73.0 0.3 while.19
  73.3 0.2 dynamic-update-slice.5
  73.5 0.1 fusion.44
  73.6 11.4 %all-reduce.9 = (f32[256]{0:T(256)S(1)}, f32[256]{0:T(256)S(1)}) all-reduce(f32[256]{0:T(256)S(1)} %dynamic-update-slice.5, f32[256]{0:T(256)S(1)} %get-tuple-element.207), channel_id=8, replica_groups=mesh['section'=4,'dp'=4,'mp'=2] {'section'}, use_global_device_ids=true, to_apply=%add.7 | all-reduce | flops 512 | bytes 4096
  85.2 0.1 reshape_squeeze.3
  85.3 0.1 sub.97
  85.5 0.1 fusion.26
  85.6 0.1 reshape.86
  85.7 0.1 subtract_multiply_fusion
  85.8 7.1 %fusion.7 = f32[64,4096]{1,0:T(8,128)} fusion(bf16[1,4096,1024]{2,1,0:T(8,128)(2,1)} %param.10, f32[64,1024]{1,0:T(8,128)S(1)} %get-tuple-element.212, f32[64]{0:T(128)S(1)} %get-tuple-element.209, f32[64]{0:T(128)S(1)} %subtract_multiply_fusion, s32[1024]{0:T(1024)S(1)} %iota_add_fusion, s32[64]{0:T(128)S(1)} %all-reduce.4), kind=kOutput, calls=%fused_computation.10 | convolution fusion | flops 537264128 | bytes 9704192 | tf_op jit(solution)/shard_map/dot_general | solution.py:117
  92.9 0.6 dynamic-slice_bitcast_fusion
  93.4 0.6 dynamic-slice_bitcast_fusion.1
  94.0 31.9 %reduce-scatter.2.cloned.1.call-done = f32[8,4096]{1,0:T(8,128)} async-done(((f32[64,4096]{1,0:T(8,128)}), f32[8,4096]{1,0:T(8,128)}) %reduce-scatter.2.cloned.1.call-update) | async-done | bytes 131088 | tf_op jit(solution)/shard_map/reduce_scatter | solution.py:116
  125.9 1.5 %fusion.20 = bf16[1,8,1,4096]{3,1,2,0:T(8,128)(2,1)} fusion(f32[8,4096]{1,0:T(8,128)} %reduce-scatter.2.cloned.1.call-done, f32[]{:T(128)S(6)} %convert_element_type.24), kind=kLoop, calls=%fused_computation.27 | loop fusion | flops 65536 | bytes 196612 | tf_op jit(solution)/shard_map/reshape | solution.py:125
  (33 shorter events, 0.7 us)
Async XLA Ops:
  7.2 65.6 %copy-start = (bf16[1,4096]{1,0:T(2,128)(2,1)S(1)}, bf16[1,4096]{1,0:T(2,128)(2,1)}, u32[]{:S(2)}) copy-start(bf16[1,4096]{1,0:T(2,128)(2,1)} %param.11) | copy-start | bytes 24580
  7.2 118.7 %reduce-scatter.2.cloned.1.call-start = ((), (), s32[]{:S(2)}) async-start(), calls=%async_computation.1 | async-start | bytes 1179648 | tf_op jit(solution)/shard_map/reduce_scatter | solution.py:116
  50.8 20.4 %copy-start.2 = (u32[32]{0:T(128)S(1)}, u32[32]{0:T(128)}, u32[]{:S(2)}) copy-start(u32[32]{0:T(128)} %constant.151) | copy-start | bytes 388
  50.8 21.6 %copy-start.1 = (s32[4]{0:T(128)S(1)}, s32[4]{0:T(128)}, u32[]{:S(2)}) copy-start(s32[4]{0:T(128)} %param.9) | copy-start | bytes 52
Sparse Core Ops, SparseCore 0:
  93.0 32.8 reduce-scatter.1
